TPU v7x, 32 devices: a whole 2x2x4 slice. The times are simulated.
32 devices in a mesh: gx: 8 (over y, x, core), gy: 4 (over z).
Axes of the slice: x: 2, y: 2, z: 4, core: 2. Of those that a mesh axis runs over, the one named last changes fastest.
Arguments:
- right_side: float32 [3, 128, 32, 256], P(None, 'gx', 'gy'), may hold values from -12 to 12
- labels: int32 [128, 32, 256], P('gx', 'gy'), may hold values 0 or 1
Outputs:
- solution: float32 [3, 128, 32, 256], P(None, 'gx', 'gy')
- residual: float32 [3, 128, 32, 256], P(None, 'gx', 'gy')
All inputs are finite; a program needn't handle non-finite values. No bound on the sum of `labels` on one device may be relied on, other than what follows from the above.
Results may differ from a plain program's by a relative error of at most 0.0003.
Values sent between devices are 32-bit elements; how exact they have to be, the bound alone decides.
A program may use at most 64 MiB of HBM per device.

v0:
```python
import math

import jax
import jax.numpy as jnp
import numpy as np
from jax import lax
from jax.sharding import PartitionSpec as P

ITERS = 4


LAMBDA_SOFT = 0.5769231
LAMBDA_RISE = 1.6452991
SHEAR_SOFT = 0.3846154
SHEAR_RISE = 2.9487179
KAPPA = 0.05


def shifted(shard, axis, by):
    size = lax.axis_size(axis)
    return lax.ppermute(shard, axis, [(i, (i + by) % size) for i in range(size)])


def corner_bits(corner):
    return (corner >> 2 & 1, corner >> 1 & 1, corner & 1)


def element_tables():
    gauss_offset = 0.5 / math.sqrt(3.0)
    gauss_points = [0.5 - gauss_offset, 0.5 + gauss_offset]
    lame_table = np.zeros((24, 24))
    shear_table = np.zeros((24, 24))
    normal_block = np.zeros((6, 6))
    normal_block[:3, :3] = 1.0
    shear_block = np.zeros((6, 6))
    for entry in range(6):
        shear_block[entry, entry] = 2.0 if entry < 3 else 1.0
    for point_x in gauss_points:
        for point_y in gauss_points:
            for point_z in gauss_points:
                strain = np.zeros((6, 24))
                for corner in range(8):
                    cx_bit, cy_bit, cz_bit = corner_bits(corner)
                    shape_x = point_x if cx_bit else 1.0 - point_x
                    shape_y = point_y if cy_bit else 1.0 - point_y
                    shape_z = point_z if cz_bit else 1.0 - point_z
                    slope_x = 1.0 if cx_bit else -1.0
                    slope_y = 1.0 if cy_bit else -1.0
                    slope_z = 1.0 if cz_bit else -1.0
                    grad_x = slope_x * shape_y * shape_z
                    grad_y = shape_x * slope_y * shape_z
                    grad_z = shape_x * shape_y * slope_z
                    column = 3 * corner
                    strain[0, column] = grad_x
                    strain[1, column + 1] = grad_y
                    strain[2, column + 2] = grad_z
                    strain[3, column + 1] = grad_z
                    strain[3, column + 2] = grad_y
                    strain[4, column] = grad_z
                    strain[4, column + 2] = grad_x
                    strain[5, column] = grad_y
                    strain[5, column + 1] = grad_x
                lame_table += 0.125 * strain.T @ normal_block @ strain
                shear_table += 0.125 * strain.T @ shear_block @ strain
    return np.concatenate([lame_table, shear_table], 0).astype(np.float32)


def table_diagonal(table):
    return np.array([table[entry, entry] for entry in range(24)], dtype=np.float32)


def moduli(labels):
    stiff = labels.astype(jnp.float32)
    return (LAMBDA_SOFT + LAMBDA_RISE * stiff, SHEAR_SOFT + SHEAR_RISE * stiff)


def element_terms(node_values, lame_block, shear_part, stiffness):
    planes, columns, depth = lame_block.shape
    rolled_z = jnp.roll(node_values, -1, 3)
    corner_views = []
    for corner in range(8):
        cx_bit, cy_bit, cz_bit = corner_bits(corner)
        source_nodes = rolled_z if cz_bit else node_values
        corner_views.append(source_nodes[:, cx_bit : cx_bit + planes, cy_bit : cy_bit + columns, :])
    stacked = jnp.concatenate(corner_views, 0).reshape(24, -1)
    products = jnp.dot(
        stiffness, stacked, precision=lax.Precision.HIGHEST, preferred_element_type=jnp.float32
    )
    forces = lame_block.reshape(1, -1) * products[:24] + shear_part.reshape(1, -1) * products[24:]
    return forces.reshape(8, 3, planes, columns, depth)


def diagonal_terms(lame_block, shear_part, diag_lame, diag_shear):
    planes, columns, depth = lame_block.shape
    forces = (
        lame_block[None] * diag_lame[:, None, None, None]
        + shear_part[None] * diag_shear[:, None, None, None]
    )
    return forces.reshape(8, 3, planes, columns, depth)


def assemble_corners(forces):
    assembled = None
    for corner in range(8):
        cx_bit, cy_bit, cz_bit = corner_bits(corner)
        portion = forces[corner]
        if cz_bit:
            portion = jnp.roll(portion, 1, 3)
        portion = jnp.pad(portion, ((0, 0), (cx_bit, 1 - cx_bit), (cy_bit, 1 - cy_bit), (0, 0)))
        assembled = portion if assembled is None else assembled + portion
    return assembled


def sweep_blocks(block_nodes, first_plane, block_count, block_width):

    def advance(carry, number):
        portion = block_nodes(number * block_width, block_width)
        portion = portion.at[:, 0].add(carry)
        return (portion[:, block_width], portion[:, :block_width])

    last_plane, pieces = lax.scan(advance, first_plane, jnp.arange(block_count, dtype=jnp.int32))
    assembled = jnp.moveaxis(pieces, 0, 1)
    assembled = assembled.reshape((3, block_count * block_width) + assembled.shape[3:])
    return (assembled, last_plane)


def fold_back(assembled, last_plane):
    arrived = shifted(last_plane, "gx", 1)
    assembled = assembled.at[:, 0].add(arrived)
    edge_index = assembled.shape[2] - 1
    column_in = shifted(assembled[:, :, edge_index], "gy", 1)
    assembled = assembled.at[:, :, 0].add(column_in)
    return assembled[:, :, :edge_index]


def owned_nodes(terms, block_count, block_width, plane_shape):

    def block_nodes(offset, planes):
        return assemble_corners(terms(offset, planes))

    first_plane = jnp.zeros(plane_shape, jnp.float32)
    assembled, last_plane = sweep_blocks(block_nodes, first_plane, block_count, block_width)
    return fold_back(assembled, last_plane)


def descent_sum(residual, scaled):
    return lax.psum(jnp.sum(residual * scaled), ("gx", "gy"))


def local(right_side, labels):
    tables = element_tables()
    stiffness = jnp.asarray(tables, dtype=jnp.float32)
    diag_lame = jnp.asarray(table_diagonal(tables[:24]), dtype=jnp.float32)
    diag_shear = jnp.asarray(table_diagonal(tables[24:]), dtype=jnp.float32)
    count_x = right_side.shape[1]
    count_y = right_side.shape[2]
    depth = right_side.shape[3]
    block_width = math.gcd(count_x, 4)
    block_count = count_x // block_width
    lame_first, shear_modulus = moduli(labels)
    plane_shape = (3, count_y + 1, depth)

    def diag_block(offset, planes):
        return diagonal_terms(
            lax.dynamic_slice_in_dim(lame_first, offset, planes, 0),
            lax.dynamic_slice_in_dim(shear_modulus, offset, planes, 0),
            diag_lame,
            diag_shear,
        )

    diagonal = owned_nodes(diag_block, block_count, block_width, plane_shape) + KAPPA
    solution = jnp.zeros_like(right_side)
    residual = right_side
    scaled = residual / diagonal
    direction = scaled
    descent = descent_sum(residual, scaled)
    for iteration in range(ITERS):
        upper_plane = shifted(direction[:, :1], "gx", -1)
        extended = jnp.concatenate([direction, upper_plane], 1)
        upper_column = shifted(extended[:, :, :1], "gy", -1)
        extended = jnp.concatenate([extended, upper_column], 2)

        def force_block(offset, planes):
            return element_terms(
                lax.dynamic_slice_in_dim(extended, offset, planes + 1, 1),
                lax.dynamic_slice_in_dim(lame_first, offset, planes, 0),
                lax.dynamic_slice_in_dim(shear_modulus, offset, planes, 0),
                stiffness,
            )

        image_vector = (
            owned_nodes(force_block, block_count, block_width, plane_shape) + KAPPA * direction
        )
        curve = lax.psum(jnp.sum(direction * image_vector), ("gx", "gy"))
        step_length = descent / curve
        solution = solution + step_length * direction
        residual = residual - step_length * image_vector
        if iteration + 1 < ITERS:
            scaled = residual / diagonal
            descent_new = descent_sum(residual, scaled)
            direction = scaled + descent_new / descent * direction
            descent = descent_new
    return (solution, residual)


def solution(mesh):
    in_specs = (P(None, "gx", "gy", None), P("gx", "gy", None))
    out_specs = (P(None, "gx", "gy", None), P(None, "gx", "gy", None))
    return jax.shard_map(local, mesh=mesh, in_specs=in_specs, out_specs=out_specs, check_vma=False)
```

profile of v0, /device:TPU:0, one launch (start us, length us, event | category | flops | bytes accessed | tf_op | source)
XLA Modules:
  0.0 497.5 jit_solution(1301822050732928141)
XLA Ops:
  1.6 11.0 %while.90 = (s32[]{:T(128)}, f32[3,9,256]{2,1,0:T(8,128)S(1)}, f32[4,3,4,9,256]{4,3,1,2,0:T(8,128)S(1)}, s32[4]{0:T(128)S(1)}, f32[16,8,256]{2,1,0:T(8,128)S(1)}...) while((s32[]{:T(128)}, f32[3,9,256]{2,1,0:T(8,128)S(1)}, ...), condition=%wide.region_1.2_spmd.clone, body=%wide.region_0.1_spmd.sunk.clone.sunk | while | flops 297990 | bytes 1946535 | solution.py:121
  13.5 4.3 collective-permute-done
  17.9 2.4 collective-permute-start.1
  20.3 4.1 collective-permute-done.1
  24.7 1.5 collective-permute-done.2
  26.2 2.0 collective-permute-start.3
  28.2 3.1 collective-permute-done.3
  31.4 1.0 broadcast.413.clone.1
  32.4 23.3 %while.91 = (s32[]{:T(128)}, f32[3,9,256]{2,1,0:T(8,128)S(1)}, f32[4,3,4,9,256]{4,3,2,1,0:T(8,128)}, s32[4]{0:T(128)S(1)}, f32[16,8,256]{2,1,0:T(8,128)S(1)}, /*...) while((s32[]{:T(128)}, f32[3,9,256]{2,1,0:T(8,128)S(1)}, ...), condition=%wide.region_5.6_spmd.clone, body=%wide.region_4.5_spmd.sunk.clone.sunk | while | flops 115150856 | bytes 15201548 | solution.py:121
  35.0 1.4 fusion.152
  40.8 1.4 fusion.152
  46.6 1.4 fusion.152
  52.4 1.4 fusion.152
  55.9 1.4 copy.42
  57.5 2.6 collective-permute-done.4
  60.3 5.9 %collective-permute-done.5 = f32[3,16,256]{2,1,0:T(8,128)S(1)} collective-permute-done((f32[3,16,256]{2,1,0:T(8,128)S(1)}, f32[3,16,256]{2,1,0:T(8,128)S(1)}, u32[]{:S(2)}, u32[]{:S(2)}) %collective-permute-start.5) | collective-permute-done | bytes 49184 | tf_op jit(solution)/shard_map/ppermute | solution.py:21
  67.0 37.3 %all-reduce.40 = (f32[]{:T(128)}, f32[]{:T(128)}) all-reduce(f32[]{:T(128)} %get-tuple-element.869, f32[]{:T(128)} %get-tuple-element.868), channel_id=1, replica_groups=mesh['gx'=8,'gy'=4] {'gx','gy'}, use_global_device_ids=true, to_apply=%region_3.4 | all-reduce | flops 2 | bytes 16 | tf_op jit(solution)/shard_map/psum | solution.py:147
  106.6 42.3 %psum.58 = f32[]{:T(128)} all-reduce(f32[]{:T(128)} %get-tuple-element.944), channel_id=1, replica_groups=mesh['gx'=8,'gy'=4] {'gx','gy'}, use_global_device_ids=true, to_apply=%region_9.10 | all-reduce | flops 1 | bytes 8 | tf_op jit(solution)/shard_map/psum | solution.py:147
  150.4 1.2 collective-permute-start.6
  151.6 1.5 collective-permute-done.6
  153.1 1.8 collective-permute-start.7
  154.9 2.8 collective-permute-done.7
  157.8 1.0 broadcast.413.clone.2
  158.8 26.3 %while.92 = (s32[]{:T(128)}, f32[3,9,256]{2,1,0:T(8,128)S(1)}, f32[4,3,4,9,256]{4,3,2,1,0:T(8,128)}, s32[4]{0:T(128)S(1)}, f32[16,8,256]{2,1,0:T(8,128)S(1)}, /*...) while((s32[]{:T(128)}, f32[3,9,256]{2,1,0:T(8,128)S(1)}, ...), condition=%wide.region_11.12_spmd.clone, body=%wide.region_10.11_spmd.sunk.clone.sunk | while | flops 115150856 | bytes 17298812 | solution.py:121
  161.3 1.4 fusion.164
  167.9 1.4 fusion.164
  174.5 1.4 fusion.164
  181.1 1.4 fusion.164
  185.6 1.5 copy.46
  187.2 2.3 collective-permute-done.8
  189.8 5.9 %collective-permute-done.9 = f32[3,16,256]{2,1,0:T(8,128)S(1)} collective-permute-done((f32[3,16,256]{2,1,0:T(8,128)S(1)}, f32[3,16,256]{2,1,0:T(8,128)S(1)}, u32[]{:S(2)}, u32[]{:S(2)}) %collective-permute-start.9) | collective-permute-done | bytes 49184 | tf_op jit(solution)/shard_map/ppermute | solution.py:21
  196.4 37.3 %psum.59 = f32[]{:T(128)} all-reduce(f32[]{:T(128)} %multiply_reduce_fusion.4), channel_id=1, replica_groups=mesh['gx'=8,'gy'=4] {'gx','gy'}, use_global_device_ids=true, to_apply=%region_13.14 | all-reduce | flops 1 | bytes 8 | tf_op jit(solution)/shard_map/psum | solution.py:194
  235.8 42.7 %psum.60 = f32[]{:T(128)} all-reduce(f32[]{:T(128)} %get-tuple-element.942), channel_id=1, replica_groups=mesh['gx'=8,'gy'=4] {'gx','gy'}, use_global_device_ids=true, to_apply=%region_15.16 | all-reduce | flops 1 | bytes 8 | tf_op jit(solution)/shard_map/psum | solution.py:147
  279.9 1.2 collective-permute-start.10
  281.1 1.5 collective-permute-done.10
  282.6 1.8 collective-permute-start.11
  284.4 3.0 collective-permute-done.11
  287.6 1.0 broadcast.413.clone.3
  288.5 26.8 %while.93 = (s32[]{:T(128)}, f32[3,9,256]{2,1,0:T(8,128)S(1)}, f32[4,3,4,9,256]{4,3,2,1,0:T(8,128)}, s32[4]{0:T(128)S(1)}, f32[16,8,256]{2,1,0:T(8,128)S(1)}, /*...) while((s32[]{:T(128)}, f32[3,9,256]{2,1,0:T(8,128)S(1)}, ...), condition=%wide.region_17.18_spmd.clone, body=%wide.region_16.17_spmd.sunk.clone.sunk | while | flops 115150856 | bytes 17298812 | solution.py:121
  291.2 1.4 fusion.176
  297.9 1.4 fusion.176
  304.6 1.4 fusion.176
  311.3 1.4 fusion.176
  315.5 1.5 copy.49
  317.2 2.5 collective-permute-done.12
  320.0 5.9 %collective-permute-done.13 = f32[3,16,256]{2,1,0:T(8,128)S(1)} collective-permute-done((f32[3,16,256]{2,1,0:T(8,128)S(1)}, f32[3,16,256]{2,1,0:T(8,128)S(1)}, u32[]{:S(2)}, u32[]{:S(2)}) %collective-permute-start.13) | collective-permute-done | bytes 49184 | tf_op jit(solution)/shard_map/ppermute | solution.py:21
  326.6 37.4 %psum.61 = f32[]{:T(128)} all-reduce(f32[]{:T(128)} %multiply_reduce_fusion.2), channel_id=1, replica_groups=mesh['gx'=8,'gy'=4] {'gx','gy'}, use_global_device_ids=true, to_apply=%region_19.20 | all-reduce | flops 1 | bytes 8 | tf_op jit(solution)/shard_map/psum | solution.py:194
  366.1 42.0 %psum.62 = f32[]{:T(128)} all-reduce(f32[]{:T(128)} %get-tuple-element.940), channel_id=1, replica_groups=mesh['gx'=8,'gy'=4] {'gx','gy'}, use_global_device_ids=true, to_apply=%region_21.22 | all-reduce | flops 1 | bytes 8 | tf_op jit(solution)/shard_map/psum | solution.py:147
  409.7 1.2 collective-permute-start.14
  410.9 1.5 collective-permute-done.14
  412.4 1.8 collective-permute-start.15
  414.2 3.0 collective-permute-done.15
  417.3 1.0 broadcast.413
  418.3 26.9 %while.94 = (s32[]{:T(128)}, f32[3,9,256]{2,1,0:T(8,128)S(1)}, f32[4,3,4,9,256]{4,3,2,1,0:T(8,128)}, s32[4]{0:T(128)S(1)}, f32[16,8,256]{2,1,0:T(8,128)S(1)}, /*...) while((s32[]{:T(128)}, f32[3,9,256]{2,1,0:T(8,128)S(1)}, ...), condition=%wide.region_23.24_spmd.clone, body=%wide.region_22.23_spmd.sunk.clone.sunk | while | flops 115150856 | bytes 17298812 | solution.py:121
  421.0 1.4 fusion.188
  427.8 1.4 fusion.188
  434.5 1.4 fusion.188
  441.2 1.4 fusion.188
  445.5 1.5 copy.52
  447.2 2.5 collective-permute-done.16
  449.9 5.9 %collective-permute-done.17 = f32[3,16,256]{2,1,0:T(8,128)S(1)} collective-permute-done((f32[3,16,256]{2,1,0:T(8,128)S(1)}, f32[3,16,256]{2,1,0:T(8,128)S(1)}, u32[]{:S(2)}, u32[]{:S(2)}) %collective-permute-start.17) | collective-permute-done | bytes 49184 | tf_op jit(solution)/shard_map/ppermute | solution.py:21
  456.6 37.3 %psum.63 = f32[]{:T(128)} all-reduce(f32[]{:T(128)} %multiply_reduce_fusion), channel_id=1, replica_groups=mesh['gx'=8,'gy'=4] {'gx','gy'}, use_global_device_ids=true, to_apply=%region_25.26 | all-reduce | flops 1 | bytes 8 | tf_op jit(solution)/shard_map/psum | solution.py:194
  495.6 1.0 copy.54
  496.5 1.0 copy.55
  (844 shorter events, 87.2 us)
Async XLA Ops:
  12.6 11.8 %copy-start.22 = (f32[3,16,8,256]{3,2,1,0:T(8,128)S(1)}, f32[3,16,8,256]{3,2,1,0:T(8,128)}, u32[]{:S(2)}) copy-start(f32[3,16,8,256]{3,2,1,0:T(8,128)} %param.45) | copy-start | bytes 1179652
  12.7 5.1 %collective-permute-start = (f32[3,9,256]{2,0,1:T(4,128)S(1)}, f32[3,9,256]{2,0,1:T(4,128)S(1)}, u32[]{:S(2)}, u32[]{:S(2)}) collective-permute-start(f32[3,9,256]{2,0,1:T(4,128)S(1)} %copy.38), channel_id=1, source_target_pairs={{0,4},{4,8},{8,12},{12,16},{16,20},{20,24},{24,28},{28,0},{1,5},{5... | collective-permute-start | bytes 82952 | tf_op jit(solution)/shard_map/ppermute | solution.py:21
  17.9 6.5 %collective-permute-start.1 = (f32[3,16,256]{2,1,0:T(8,128)S(1)}, f32[3,16,256]{2,1,0:T(8,128)S(1)}, u32[]{:S(2)}, u32[]{:S(2)}) collective-permute-start(f32[3,16,256]{2,1,0:T(8,128)S(1)} %slice_bitcast_fusion.15), channel_id=1, source_target_pairs={{0,1},{1,2},{2,3},{3,0},{4,5},{5,6},{6,7},{7,4},{8,9},{9,10},{10,1... | collective-permute-start | bytes 147464 | tf_op jit(solution)/shard_map/ppermute | solution.py:21
  24.4 8.0 %copy-start.5 = (f32[48,24]{1,0:T(8,128)S(1)}, f32[48,24]{1,0:T(8,128)}, u32[]{:S(2)}) copy-start(f32[48,24]{1,0:T(8,128)} %constant.564.clone..sunk.8) | copy-start | bytes 13828
  24.6 1.6 collective-permute-start.2
  26.2 5.1 %collective-permute-start.3 = (f32[3,17,1,256]{3,1,0,2:T(8,128)S(1)}, f32[3,17,1,256]{3,1,0,2:T(8,128)S(1)}, u32[]{:S(2)}, u32[]{:S(2)}) collective-permute-start(f32[3,17,1,256]{3,1,0,2:T(8,128)S(1)} %pad_maximum_fusion.12), channel_id=1, source_target_pairs={{0,3},{1,0},{2,1},{3,2},{4,7},{5,4},{6,5},{7,6},{8,11},{9,8},{10,9... | collective-permute-start | bytes 156680 | tf_op jit(solution)/shard_map/ppermute | solution.py:21
  55.7 10.5 %copy-start.23 = (f32[3,16,8,256]{3,2,1,0:T(8,128)S(1)}, f32[3,16,8,256]{3,2,1,0:T(8,128)}, u32[]{:S(2)}) copy-start(f32[3,16,8,256]{3,2,1,0:T(8,128)} %param.45) | copy-start | bytes 1179652
  55.7 4.3 collective-permute-start.4
  60.3 5.9 %collective-permute-start.5 = (f32[3,16,256]{2,1,0:T(8,128)S(1)}, f32[3,16,256]{2,1,0:T(8,128)S(1)}, u32[]{:S(2)}, u32[]{:S(2)}) collective-permute-start(f32[3,16,256]{2,1,0:T(8,128)S(1)} %slice_bitcast_fusion.14), channel_id=1, source_target_pairs={{0,1},{1,2},{2,3},{3,0},{4,5},{5,6},{6,7},{7,4},{8,9},{9,10},{10,1... | collective-permute-start | bytes 147464 | tf_op jit(solution)/shard_map/ppermute | solution.py:21
  106.6 48.3 %copy-start.20 = (f32[3,16,8,256]{3,1,0,2:T(8,128)}, f32[3,16,8,256]{3,1,0,2:T(8,128)S(1)}, u32[]{:S(2)}) copy-start(f32[3,16,8,256]{3,1,0,2:T(8,128)S(1)} %get-tuple-element.945) | copy-start | bytes 1179652
  150.4 2.7 collective-permute-start.6
  153.1 4.6 collective-permute-start.7
  158.8 1.8 copy-start.6
  158.8 2.5 copy-start.12
  164.1 1.2 copy-start.7
  164.1 1.2 copy-start.13
  165.4 1.8 copy-start.6
  165.4 2.5 copy-start.12
  172.0 1.8 copy-start.6
  172.0 2.5 copy-start.12
  178.5 1.8 copy-start.6
  178.5 2.5 copy-start.12
  183.9 1.2 copy-start.13
  185.2 4.3 collective-permute-start.8
  185.6 49.4 %copy-start.21 = (f32[3,16,8,256]{3,1,0,2:T(8,128)S(1)}, f32[3,16,8,256]{3,1,0,2:T(8,128)}, u32[]{:S(2)}) copy-start(f32[3,16,8,256]{3,1,0,2:T(8,128)} %copy-done.20) | copy-start | bytes 1179652
  189.7 5.9 %collective-permute-start.9 = (f32[3,16,256]{2,1,0:T(8,128)S(1)}, f32[3,16,256]{2,1,0:T(8,128)S(1)}, u32[]{:S(2)}, u32[]{:S(2)}) collective-permute-start(f32[3,16,256]{2,1,0:T(8,128)S(1)} %slice_bitcast_fusion.13), channel_id=1, source_target_pairs={{0,1},{1,2},{2,3},{3,0},{4,5},{5,6},{6,7},{7,4},{8,9},{9,10},{10,1... | collective-permute-start | bytes 147464 | tf_op jit(solution)/shard_map/ppermute | solution.py:21
  235.8 51.8 %copy-start.18 = (f32[3,16,8,256]{3,1,0,2:T(8,128)}, f32[3,16,8,256]{3,1,0,2:T(8,128)S(1)}, u32[]{:S(2)}) copy-start(f32[3,16,8,256]{3,1,0,2:T(8,128)S(1)} %get-tuple-element.943) | copy-start | bytes 1179652
  279.9 8.7 %copy-start = (f32[3,16,8,256]{3,1,0,2:T(8,128)}, f32[3,16,8,256]{3,1,0,2:T(8,128)S(1)}, u32[]{:S(2)}) copy-start(f32[3,16,8,256]{3,1,0,2:T(8,128)S(1)} %multiply_add_fusion.3) | copy-start | bytes 1179652
  279.9 2.7 collective-permute-start.10
  282.6 4.8 collective-permute-start.11
  288.5 1.9 copy-start.8
  288.6 2.6 copy-start.14
  294.0 1.2 copy-start.9
  294.0 1.2 copy-start.15
  295.2 1.9 copy-start.8
  295.3 2.6 copy-start.14
  301.9 1.9 copy-start.8
  301.9 2.6 copy-start.14
  308.6 1.9 copy-start.8
  308.6 2.6 copy-start.14
  314.1 1.2 copy-start.15
  315.3 10.5 %copy-start.1 = (f32[3,16,8,256]{3,1,0,2:T(8,128)S(1)}, f32[3,16,8,256]{3,1,0,2:T(8,128)}, u32[]{:S(2)}) copy-start(f32[3,16,8,256]{3,1,0,2:T(8,128)} %copy-done) | copy-start | bytes 1179652
  315.3 4.3 collective-permute-start.12
  315.5 49.8 %copy-start.19 = (f32[3,16,8,256]{3,1,0,2:T(8,128)S(1)}, f32[3,16,8,256]{3,1,0,2:T(8,128)}, u32[]{:S(2)}) copy-start(f32[3,16,8,256]{3,1,0,2:T(8,128)} %copy-done.18) | copy-start | bytes 1179652
  319.9 5.9 %collective-permute-start.13 = (f32[3,16,256]{2,1,0:T(8,128)S(1)}, f32[3,16,256]{2,1,0:T(8,128)S(1)}, u32[]{:S(2)}, u32[]{:S(2)}) collective-permute-start(f32[3,16,256]{2,1,0:T(8,128)S(1)} %slice_bitcast_fusion.12), channel_id=1, source_target_pairs={{0,1},{1,2},{2,3},{3,0},{4,5},{5,6},{6,7},{7,4},{8,9},{9,10},{10,1... | collective-permute-start | bytes 147464 | tf_op jit(solution)/shard_map/ppermute | solution.py:21
  366.1 51.2 %copy-start.24 = (f32[3,16,8,256]{3,1,0,2:T(8,128)}, f32[3,16,8,256]{3,1,0,2:T(8,128)S(1)}, u32[]{:S(2)}) copy-start(f32[3,16,8,256]{3,1,0,2:T(8,128)S(1)} %get-tuple-element.941) | copy-start | bytes 1179652
  409.6 8.7 %copy-start.3 = (f32[3,16,8,256]{3,1,0,2:T(8,128)}, f32[3,16,8,256]{3,1,0,2:T(8,128)S(1)}, u32[]{:S(2)}) copy-start(f32[3,16,8,256]{3,1,0,2:T(8,128)S(1)} %multiply_add_fusion.2) | copy-start | bytes 1179652
  409.7 2.7 collective-permute-start.14
  412.4 4.8 collective-permute-start.15
  418.3 2.0 copy-start.10
  418.3 2.7 copy-start.16
  423.9 1.2 copy-start.11
  423.9 1.2 copy-start.17
  425.1 2.0 copy-start.10
  425.1 2.7 copy-start.16
  431.8 2.0 copy-start.10
  431.8 2.7 copy-start.16
  438.5 2.0 copy-start.10
  438.6 2.7 copy-start.16
  445.3 10.5 %copy-start.4 = (f32[3,16,8,256]{3,1,0,2:T(8,128)S(1)}, f32[3,16,8,256]{3,1,0,2:T(8,128)}, u32[]{:S(2)}) copy-start(f32[3,16,8,256]{3,1,0,2:T(8,128)} %copy-done.3) | copy-start | bytes 1179652
  445.3 4.3 collective-permute-start.16
  445.5 49.8 %copy-start.2 = (f32[3,16,8,256]{3,1,0,2:T(8,128)S(1)}, f32[3,16,8,256]{3,1,0,2:T(8,128)}, u32[]{:S(2)}) copy-start(f32[3,16,8,256]{3,1,0,2:T(8,128)} %copy-done) | copy-start | bytes 1179652
  445.5 49.8 %copy-start.25 = (f32[3,16,8,256]{3,1,0,2:T(8,128)S(1)}, f32[3,16,8,256]{3,1,0,2:T(8,128)}, u32[]{:S(2)}) copy-start(f32[3,16,8,256]{3,1,0,2:T(8,128)} %copy-done.24) | copy-start | bytes 1179652
  449.9 5.9 %collective-permute-start.17 = (f32[3,16,256]{2,1,0:T(8,128)S(1)}, f32[3,16,256]{2,1,0:T(8,128)S(1)}, u32[]{:S(2)}, u32[]{:S(2)}) collective-permute-start(f32[3,16,256]{2,1,0:T(8,128)S(1)} %slice_bitcast_fusion.11), channel_id=1, source_target_pairs={{0,1},{1,2},{2,3},{3,0},{4,5},{5,6},{6,7},{7,4},{8,9},{9,10},{10,1... | collective-permute-start | bytes 147464 | tf_op jit(solution)/shard_map/ppermute | solution.py:21
  (16 other events, 19.1 us)
where the time goes:
time: 500 us; the launch traced here: 498 us
  blocking collectives  276 us (55%)
  local copies, waits for them, and re-layouts  76.6 us (15%)
  waiting for transfers between devices  59.8 us (12%)
  matrix products  21.8 us (4%)
  other arithmetic  20.5 us (4%)
  loops' own time  16.7 us (3%)
  starting transfers between devices  15.2 us (3%)
  between operations  10.5 us (2%)
    psum x4, blocking collectives, descent_sum(): return lax.psum(jnp.sum(residual * scaled), ('gx', 'gy'))  164 us
    psum x3, blocking collectives, local(): curve = lax.psum(jnp.sum(direction * image_vector), ('gx', 'gy'))  112 us
    ppermute x18, waiting for transfers between devices, shifted(): lax.ppermute(shard, axis, [(i, (i + by) % size) for i in range(size)])  59.8 us
    while x384, local copies, waits for them, and re-layouts  22.8 us
    dot_general x16, matrix products, element_terms(): jnp.dot(stiffness, stacked, precision=lax.Precision.HIGHEST, preferred_el...  21.8 us
    another operation x5, loops' own time, sweep_blocks(): lax.scan(advance, first_plane, jnp.arange(block_count, dtype=jnp.int32))  16.7 us
    ppermute x18, starting transfers between devices, shifted(): lax.ppermute(shard, axis, [(i, (i + by) % size) for i in range(size)])  15.2 us
    dynamic_slice x20, local copies, waits for them, and re-layouts, sweep_blocks(): lax.scan(advance, first_plane, jnp.arange(block_count, dtype=jnp.int32))  12.4 us
  transfers between devices with their start and end apart: 18, of which 18 were waited for; matrix products, arithmetic and copies ran while one was open for 1% of the time, Pallas kernels for 0%

commit v1 on v0

v1 whole, which is shorter than its diff:
```python
import functools
import math

import jax
import jax.numpy as jnp
import numpy as np
from jax import lax
from jax.experimental import pallas as pl
from jax.experimental.pallas import tpu as pltpu
from jax.sharding import PartitionSpec as P

ITERS = 4

LAMBDA_SOFT = 0.5769231
LAMBDA_RISE = 1.6452991
SHEAR_SOFT = 0.3846154
SHEAR_RISE = 2.9487179
KAPPA = 0.05
PIVOT_FLOOR = 1e-6
SHIFTS = (1.0, 1.4, 1.4)
MIXES = (0.0, 0.3, 0.45)

MESH = pl.DeviceIdType.MESH
F32 = jnp.float32


def corner_bits(corner):
    return (corner >> 2 & 1, corner >> 1 & 1, corner & 1)


def element_tables():
    gauss_offset = 0.5 / math.sqrt(3.0)
    gauss_points = [0.5 - gauss_offset, 0.5 + gauss_offset]
    lame_table = np.zeros((24, 24))
    shear_table = np.zeros((24, 24))
    normal_block = np.zeros((6, 6))
    normal_block[:3, :3] = 1.0
    shear_block = np.diag([2.0, 2.0, 2.0, 1.0, 1.0, 1.0])
    for point_x in gauss_points:
        for point_y in gauss_points:
            for point_z in gauss_points:
                strain = np.zeros((6, 24))
                for corner in range(8):
                    cx_bit, cy_bit, cz_bit = corner_bits(corner)
                    shape_x = point_x if cx_bit else 1.0 - point_x
                    shape_y = point_y if cy_bit else 1.0 - point_y
                    shape_z = point_z if cz_bit else 1.0 - point_z
                    slope_x = 1.0 if cx_bit else -1.0
                    slope_y = 1.0 if cy_bit else -1.0
                    slope_z = 1.0 if cz_bit else -1.0
                    grad_x = slope_x * shape_y * shape_z
                    grad_y = shape_x * slope_y * shape_z
                    grad_z = shape_x * shape_y * slope_z
                    column = 3 * corner
                    strain[0, column] = grad_x
                    strain[1, column + 1] = grad_y
                    strain[2, column + 2] = grad_z
                    strain[3, column + 1] = grad_z
                    strain[3, column + 2] = grad_y
                    strain[4, column] = grad_z
                    strain[4, column + 2] = grad_x
                    strain[5, column] = grad_y
                    strain[5, column + 1] = grad_x
                lame_table += 0.125 * strain.T @ normal_block @ strain
                shear_table += 0.125 * strain.T @ shear_block @ strain
    return lame_table, shear_table


def diagonal_weights():
    lame_table, shear_table = element_tables()
    lame, shear = np.diag(lame_table), np.diag(shear_table)
    assert np.allclose(lame, lame[0]) and np.allclose(shear, shear[0])
    soft = LAMBDA_SOFT * lame[0] + SHEAR_SOFT * shear[0]
    rise = LAMBDA_RISE * lame[0] + SHEAR_RISE * shear[0]
    return float(8.0 * soft + KAPPA), float(rise)


def voxel_forces(lower, upper, stiff):
    l0 = LAMBDA_SOFT / 16.0 + LAMBDA_RISE / 16.0 * stiff
    m0 = SHEAR_SOFT / 16.0 + SHEAR_RISE / 16.0 * stiff
    l1, m1 = l0 * (1.0 / 3.0), m0 * (1.0 / 3.0)
    q = (l1 + 4.0 * m1) * (1.0 / 3.0)
    m0_2 = m0 + m0
    m1_3 = m0
    fx, fy, fz, fxy, fxz, fyz, fxyz = ([None] * 3 for _ in range(7))
    ex, ey, ez, exy, exz, eyz = ([None] * 3 for _ in range(6))
    for c in range(3):
        a, b = lower[4 * c : 4 * c + 4], upper[4 * c : 4 * c + 4]
        ex[c] = b[0] - a[0]
        ey[c], exy[c] = a[1] + b[1], b[1] - a[1]
        ez[c], exz[c] = a[2] + b[2], b[2] - a[2]
        eyz[c] = a[3] + b[3]
        fxyz[c] = q * (b[3] - a[3])
    trace = l0 * (ex[0] + ey[1] + ez[2])
    fx[0] = trace + m0_2 * ex[0]
    fy[1] = trace + m0_2 * ey[1]
    fz[2] = trace + m0_2 * ez[2]
    fy[0] = fx[1] = m0 * (ey[0] + ex[1])
    fz[0] = fx[2] = m0 * (ez[0] + ex[2])
    fz[1] = fy[2] = m0 * (ez[1] + ey[2])
    part = l1 * (exy[0] + eyz[2])
    fxy[0], fyz[2] = part + m1_3 * exy[0], part + m1_3 * eyz[2]
    part = l1 * (exy[1] + exz[2])
    fxy[1], fxz[2] = part + m1_3 * exy[1], part + m1_3 * exz[2]
    part = l1 * (exz[0] + eyz[1])
    fxz[0], fyz[1] = part + m1_3 * exz[0], part + m1_3 * eyz[1]
    total = eyz[0] + exz[1] + exy[2]
    fyz[0] = m1 * (total + eyz[0])
    fxz[1] = m1 * (total + exz[1])
    fxy[2] = m1 * (total + exy[2])
    low, high = [], []
    for c in range(3):
        low += [-fx[c], fy[c] - fxy[c], fz[c] - fxz[c], fyz[c] - fxyz[c]]
        high += [fx[c], fy[c] + fxy[c], fz[c] + fxz[c], fyz[c] + fxyz[c]]
    return low, high


def cg_kernel(nx, ny, cx, cy, nz, rhs_hbm, lab_hbm, sol_ref, res_ref,
              bvec, zvec, vvec, lab, stiff, rinv, comb, forc, ysend, yrecv, csend, crecv,
              psend, precv, in_sem, send_sem, recv_sem, lsend_sem, lrecv_sem,
              rsend_sem, rrecv_sem):
    rows = cy + 8
    n = nx * ny
    gx, gy = lax.axis_index("gx"), lax.axis_index("gy")
    me = gx * ny + gy
    xs = {-1: lax.rem(gx + nx - 1, nx), 0: gx, 1: lax.rem(gx + 1, nx)}
    ys = {-1: lax.rem(gy + ny - 1, ny), 0: gy, 1: lax.rem(gy + 1, ny)}

    load_b = pltpu.make_async_copy(
        rhs_hbm, bvec.at[:, pl.ds(1, cx), pl.ds(0, cy), :], in_sem.at[0])
    load_l = pltpu.make_async_copy(
        lab_hbm, lab.at[pl.ds(2, cx), pl.ds(0, cy), :], in_sem.at[1])
    load_b.start()
    load_l.start()

    barrier = pltpu.get_barrier_semaphore()

    def greet(k, _):
        other = lax.rem(me + k, n)
        pl.semaphore_signal(barrier, inc=1, device_id=(other // ny, lax.rem(other, ny)),
                            device_id_type=MESH)
        return 0

    lax.fori_loop(1, n, greet, 0)
    load_b.wait()
    load_l.wait()

    sides = (1, -1)
    corners = ((1, 1), (1, -1), (-1, 1), (-1, -1))
    pending = []

    def remote(src, dst, s_sem, r_sem, dx, dy):
        copy = pltpu.make_async_remote_copy(
            src_ref=src, dst_ref=dst, send_sem=s_sem, recv_sem=r_sem,
            device_id=(xs[dx], ys[dy]), device_id_type=MESH)
        copy.start()
        pending.append(copy)
        return copy

    def exchange(turn, vec, depth):
        copies = []
        for k, side in enumerate(sides):
            parts = depth[k]
            copies.append(remote(ysend.at[turn, k, pl.ds(0, parts)],
                                 yrecv.at[turn, k, pl.ds(0, parts)],
                                 send_sem.at[turn, k], recv_sem.at[turn, k], 0, side))
        for k, (dx, dy) in enumerate(corners):
            copies.append(remote(csend.at[turn, k], crecv.at[turn, k],
                                 send_sem.at[turn, 4 + k], recv_sem.at[turn, 4 + k], dx, dy))
        for k, side in enumerate(sides):
            mine, theirs = (cx, 0) if side == 1 else (1, cx + 1)
            copies.append(remote(vec.at[:, pl.ds(mine, 1), pl.ds(0, cy), :],
                                 vec.at[:, pl.ds(theirs, 1), pl.ds(0, cy), :],
                                 send_sem.at[turn, 2 + k], recv_sem.at[turn, 2 + k], side, 0))
        return copies

    row_of = {1: rows - 1, -1: cy}
    plane_of = {1: 0, -1: cx + 1}

    def unpack(turn, vec):
        def body(i, _):
            for k, side in enumerate(sides):
                for c in range(3):
                    vec[c, i + 1, pl.ds(row_of[side], 1), :] = yrecv[turn, k, c, pl.ds(i, 1), :]
            return 0

        lax.fori_loop(0, cx, body, 0)
        for k, (dx, dy) in enumerate(corners):
            for c in range(3):
                vec[c, plane_of[dx], pl.ds(row_of[dy], 1), :] = crecv[turn, k, pl.ds(c, 1), :]

    def pack_first(i, _):
        for c in range(3):
            ysend[0, 0, c, pl.ds(i, 1), :] = bvec[c, i + 1, pl.ds(cy - 1, 1), :]
            ysend[0, 1, c, pl.ds(i, 1), :] = bvec[c, i + 1, pl.ds(0, 1), :]
        for e in range(2):
            ysend[0, 0, 3 + e, pl.ds(i, 1), :] = lab[i + 2, pl.ds(cy - 2 + e, 1), :].astype(F32)
        ysend[0, 1, 3, pl.ds(i, 1), :] = lab[i + 2, pl.ds(0, 1), :].astype(F32)
        stiff[i + 2, pl.ds(0, cy), :] = lab[i + 2, pl.ds(0, cy), :].astype(F32)
        return 0

    lax.fori_loop(0, cx, pack_first, 0)

    def label_spots(dx, dy):
        planes = ((cx, 0), (cx + 1, 1)) if dx == 1 else ((2, cx + 2),)
        lines = ((cy - 2, rows - 2), (cy - 1, rows - 1)) if dy == 1 else ((0, cy),)
        return [(p, q) for p in planes for q in lines]

    for k, (dx, dy) in enumerate(corners):
        plane, line = (cx if dx == 1 else 1), (cy - 1 if dy == 1 else 0)
        for c in range(3):
            csend[0, k, pl.ds(c, 1), :] = bvec[c, plane, pl.ds(line, 1), :]
        for e, (p, q) in enumerate(label_spots(dx, dy)):
            csend[0, k, pl.ds(3 + e, 1), :] = lab[p[0], pl.ds(q[0], 1), :].astype(F32)

    pl.semaphore_wait(barrier, n - 1)
    arriving = exchange(0, bvec, (5, 4))
    arriving.append(remote(stiff.at[pl.ds(cx, 2), pl.ds(0, cy), :],
                           stiff.at[pl.ds(0, 2), pl.ds(0, cy), :],
                           lsend_sem.at[0], lrecv_sem.at[0], 1, 0))
    arriving.append(remote(stiff.at[pl.ds(2, 1), pl.ds(0, cy), :],
                           stiff.at[pl.ds(cx + 2, 1), pl.ds(0, cy), :],
                           lsend_sem.at[1], lrecv_sem.at[1], -1, 0))
    for copy in arriving:
        copy.wait_recv()
    unpack(0, bvec)

    def unpack_labels(i, _):
        for e in range(2):
            stiff[i + 2, pl.ds(rows - 2 + e, 1), :] = yrecv[0, 0, 3 + e, pl.ds(i, 1), :]
        stiff[i + 2, pl.ds(cy, 1), :] = yrecv[0, 1, 3, pl.ds(i, 1), :]
        return 0

    lax.fori_loop(0, cx, unpack_labels, 0)
    for k, (dx, dy) in enumerate(corners):
        for e, (p, q) in enumerate(label_spots(dx, dy)):
            stiff[p[1], pl.ds(q[1], 1), :] = crecv[0, k, pl.ds(3 + e, 1), :]

    base, rise = diagonal_weights()

    def prepare(i, _):
        count = stiff[i] + stiff[i + 1]
        count = count + pltpu.roll(count, 1, 0)
        count = count + pltpu.roll(count, 1, 1)
        inverse = 1.0 / (base + rise * count)
        rinv[i] = inverse
        for c in range(3):
            zvec[0, c, i] = bvec[c, i] * inverse
        return 0

    lax.fori_loop(0, cx + 2, prepare, 0)

    for turn in range(ITERS):
        def combine(i, _):
            for c in range(3):
                u = zvec[turn, c, i]
                up = pltpu.roll(u, nz - 1, 1)
                s, d = u + up, up - u
                s_up, d_up = pltpu.roll(s, rows - 1, 0), pltpu.roll(d, rows - 1, 0)
                comb[i, 4 * c] = s + s_up
                comb[i, 4 * c + 1] = s_up - s
                comb[i, 4 * c + 2] = d + d_up
                comb[i, 4 * c + 3] = d_up - d
            return 0

        lax.fori_loop(0, cx + 2, combine, 0)

        for ty in range(rows // 8):
            for tz in range(nz // 128):
                tile = (pl.ds(8 * ty, 8), pl.ds(128 * tz, 128))

                def take(p):
                    return [comb[(p, m) + tile] for m in range(12)]

                first = take(0)
                second = take(1)
                _, high = voxel_forces(first, second, stiff[(1,) + tile])

                def sweep(p, carry):
                    lower, before = carry[:12], carry[12:]
                    upper = take(p + 1)
                    low, high = voxel_forces(lower, upper, stiff[(p + 1,) + tile])
                    for m in range(12):
                        forc[(p - 1, m) + tile] = before[m] + low[m]
                    return tuple(upper) + tuple(high)

                lax.fori_loop(1, cx + 1, sweep, tuple(second) + tuple(high))

        def finish(i, _):
            for c in range(3):
                g = [forc[i, 4 * c + m] for m in range(4)]
                s = (g[0] - g[1]) + pltpu.roll(g[0] + g[1], 1, 0)
                d = (g[2] - g[3]) + pltpu.roll(g[2] + g[3], 1, 0)
                s, d = s[:cy], d[:cy]
                z = zvec[turn, c, i + 1, pl.ds(0, cy), :]
                image = (s - d) + pltpu.roll(s + d, 1, 1) + KAPPA * z
                vvec[turn, c, i] = image
                if turn + 1 < ITERS:
                    new = rinv[i + 1, pl.ds(0, cy), :] * image - SHIFTS[turn] * z
                    if turn > 0:
                        new = new - MIXES[turn] * zvec[turn - 1, c, i + 1, pl.ds(0, cy), :]
                    zvec[turn + 1, c, i + 1, pl.ds(0, cy), :] = new
                    ysend[turn + 1, 0, c, pl.ds(i, 1), :] = new[cy - 1 :]
                    ysend[turn + 1, 1, c, pl.ds(i, 1), :] = new[:1]
            return 0

        lax.fori_loop(0, cx, finish, 0)
        if turn + 1 < ITERS:
            vec = zvec.at[turn + 1]
            for k, (dx, dy) in enumerate(corners):
                plane, line = (cx if dx == 1 else 1), (cy - 1 if dy == 1 else 0)
                for c in range(3):
                    csend[turn + 1, k, pl.ds(c, 1), :] = vec[c, plane, pl.ds(line, 1), :]
            arriving = exchange(turn + 1, vec, (3, 3))
            for copy in arriving:
                copy.wait_recv()
            unpack(turn + 1, vec)

    pairs = [(i, None) for i in range(ITERS)]
    pairs += [(i, j) for j in range(ITERS) for i in range(j + 1)]

    def products(i, carry):
        carry = list(carry)
        for c in range(3):
            zs = [zvec[j, c, i + 1, pl.ds(0, cy), :] for j in range(ITERS)]
            vs = [vvec[j, c, i] for j in range(ITERS)]
            right = bvec[c, i + 1, pl.ds(0, cy), :]
            for k, (a, b) in enumerate(pairs):
                term = zs[a] * (right if b is None else vs[b])
                part = term[:8, :128]
                for ty in range(cy // 8):
                    for tz in range(nz // 128):
                        if ty or tz:
                            part = part + term[8 * ty : 8 * ty + 8, 128 * tz : 128 * tz + 128]
                carry[k] = carry[k] + part
        return tuple(carry)

    sums = lax.fori_loop(0, cx, products,
                         tuple(jnp.zeros((8, 128), F32) for _ in pairs))
    lane = lax.broadcasted_iota(jnp.int32, (1, 128), 1)
    row = jnp.zeros((1, 128), F32)
    for k, part in enumerate(sums):
        line = jnp.sum(part, axis=0, keepdims=True)
        row = jnp.where(lane == k, jnp.sum(line, axis=1, keepdims=True), row)
    psend[...] = row
    precv[me] = row

    def share(k):
        other = lax.rem(me + k, n)
        return pltpu.make_async_remote_copy(
            src_ref=psend, dst_ref=precv.at[me], send_sem=rsend_sem.at[k],
            recv_sem=rrecv_sem.at[k], device_id=(other // ny, lax.rem(other, ny)),
            device_id_type=MESH)

    def start_share(k, _):
        share(k).start()
        return 0

    def end_share(k, _):
        share(k).wait()
        return 0

    lax.fori_loop(1, n, start_share, 0)
    for copy in pending:
        copy.wait_send()
    lax.fori_loop(1, n, end_share, 0)
    total = jnp.sum(precv[...], axis=0)

    picked = {}
    for k, pair in enumerate(pairs):
        picked[pair] = jnp.sum(jnp.where(lane == k, total, 0.0), axis=1, keepdims=True)

    low, inv, scaled, forward = {}, [], {}, []
    for j in range(ITERS):
        for i in range(j):
            w = picked[(i, j)]
            for m in range(i):
                w = w - low[(i, m)] * scaled[(j, m)]
            scaled[(j, i)] = w
            low[(j, i)] = w * inv[i]
        pivot = picked[(j, j)]
        rhs = picked[(j, None)]
        for m in range(j):
            pivot = pivot - low[(j, m)] * scaled[(j, m)]
            rhs = rhs - low[(j, m)] * forward[m]
        sound = pivot > PIVOT_FLOOR * picked[(j, j)]
        inv.append(jnp.where(sound, 1.0 / jnp.where(sound, pivot, 1.0), 0.0))
        forward.append(rhs)
    coef = [None] * ITERS
    for j in reversed(range(ITERS)):
        y = forward[j] * inv[j]
        for i in range(j + 1, ITERS):
            y = y - low[(i, j)] * coef[i]
        coef[j] = y
    wide = [jnp.broadcast_to(y, (cy, nz)) for y in coef]

    def write(i, _):
        for c in range(3):
            x = wide[0] * zvec[0, c, i + 1, pl.ds(0, cy), :]
            r = bvec[c, i + 1, pl.ds(0, cy), :] - wide[0] * vvec[0, c, i]
            for j in range(1, ITERS):
                x = x + wide[j] * zvec[j, c, i + 1, pl.ds(0, cy), :]
                r = r - wide[j] * vvec[j, c, i]
            sol_ref[c, i] = x
            res_ref[c, i] = r
        return 0

    lax.fori_loop(0, cx, write, 0)


def solution(mesh):
    nx, ny = mesh.shape["gx"], mesh.shape["gy"]

    def local(right_side, labels):
        _, cx, cy, nz = right_side.shape
        rows, n = cy + 8, nx * ny
        dma = pltpu.SemaphoreType.DMA
        shape = jax.ShapeDtypeStruct(right_side.shape, F32)
        return tuple(pl.pallas_call(
            functools.partial(cg_kernel, nx, ny, cx, cy, nz),
            out_shape=(shape, shape),
            in_specs=[pl.BlockSpec(memory_space=pl.ANY)] * 2,
            out_specs=(pl.BlockSpec(memory_space=pltpu.VMEM),) * 2,
            scratch_shapes=[
                pltpu.VMEM((3, cx + 2, rows, nz), F32),
                pltpu.VMEM((ITERS, 3, cx + 2, rows, nz), F32),
                pltpu.VMEM((ITERS, 3, cx, cy, nz), F32),
                pltpu.VMEM((cx + 3, rows, nz), jnp.int32),
                pltpu.VMEM((cx + 3, rows, nz), F32),
                pltpu.VMEM((cx + 2, rows, nz), F32),
                pltpu.VMEM((cx + 2, 12, rows, nz), F32),
                pltpu.VMEM((cx, 12, rows, nz), F32),
                pltpu.VMEM((ITERS, 2, 5, cx, nz), F32),
                pltpu.VMEM((ITERS, 2, 5, cx, nz), F32),
                pltpu.VMEM((ITERS, 4, 8, nz), F32),
                pltpu.VMEM((ITERS, 4, 8, nz), F32),
                pltpu.VMEM((1, 128), F32),
                pltpu.VMEM((n, 1, 128), F32),
                dma((2,)), dma((ITERS, 8)), dma((ITERS, 8)), dma((2,)), dma((2,)),
                dma((n,)), dma((n,)),
            ],
            compiler_params=pltpu.CompilerParams(
                collective_id=0, has_side_effects=True, vmem_limit_bytes=48 * 1024 * 1024),
            name="cg",
        )(right_side, labels))

    in_specs = (P(None, "gx", "gy", None), P("gx", "gy", None))
    out_specs = (P(None, "gx", "gy", None), P(None, "gx", "gy", None))
    return jax.shard_map(local, mesh=mesh, in_specs=in_specs, out_specs=out_specs, check_vma=False)
```

time: 500 us -> 62.4 us (0.12)
  blocking collectives: 276 us -> 0 us
  local copies, waits for them, and re-layouts: 76.6 us -> 3.39 us
  waiting for transfers between devices: 59.8 us -> 0 us
  Pallas kernels: 0 us -> 58.2 us
  matrix products: 21.8 us -> 0 us
  other arithmetic: 20.5 us -> 0 us
  loops' own time: 16.7 us -> 0 us
  starting transfers between devices: 15.2 us -> 0 us
  between operations: 10.5 us -> 0.65 us
    psum x7 -> x0, blocking collectives: 276 us -> none  [the longest x4 164 us: descent_sum(): return lax.psum(jnp.sum(residual * scaled), ('gx', 'gy'))]
    ppermute x18 -> x0, waiting for transfers between devices: 59.8 us -> none  [shifted(): lax.ppermute(shard, axis, [(i, (i + by) % size) for i in range(size)])]
    pallas_call x0 -> x1, Pallas kernels: none -> 58.2 us  [local(): pl.pallas_call(functools.partial(cg_kernel, nx, ny, cx, cy, nz), out_shap...]
    while x389 -> x0, local copies, waits for them, and re-layouts: 22.9 us -> none
    dot_general x16 -> x0, matrix products: 21.8 us -> none  [element_terms(): jnp.dot(stiffness, stacked, precision=lax.Precision.HIGHEST, preferred_el...]
    another operation x5 -> x0, loops' own time: 16.7 us -> none  [sweep_blocks(): lax.scan(advance, first_plane, jnp.arange(block_count, dtype=jnp.int32))]
    ppermute x18 -> x0, starting transfers between devices: 15.2 us -> none  [shifted(): lax.ppermute(shard, axis, [(i, (i + by) % size) for i in range(size)])]
    dynamic_slice x32 -> x0, local copies, waits for them, and re-layouts: 14.3 us -> none  [the longest x20 12.4 us: sweep_blocks(): lax.scan(advance, first_plane, jnp.arange(block_count, dtype=jnp.int32))]
  transfers between devices with their start and end apart: 18 -> 0, of which waited for: 18 -> 0; matrix products, arithmetic and copies ran while one was open for 1% -> 0% of each run, Pallas kernels for 0% -> 0%
where the time goes in v1:
time: 62.4 us; the launch traced here: 62.2 us
  Pallas kernels  58.2 us (93%)
  local copies, waits for them, and re-layouts  3.39 us (5%)
  between operations  0.65 us (1%)
    pallas_call x1, Pallas kernels, local(): pl.pallas_call(functools.partial(cg_kernel, nx, ny, cx, cy, nz), out_shap...  58.2 us
    unnamed x6, local copies, waits for them, and re-layouts  3.39 us

profile of v1, /device:TPU:0, one launch (start us, length us, event | category | flops | bytes accessed | tf_op | source)
XLA Modules:
  0.0 62.2 jit_solution(11378501119289772785)
XLA Ops:
  0.6 0.0 copy-start
  0.6 1.0 %copy-done = f32[3,16,8,256]{3,2,1,0:T(8,128)S(1)} copy-done((f32[3,16,8,256]{3,2,1,0:T(8,128)S(1)}, f32[3,16,8,256]{3,2,1,0:T(8,128)}, u32[]{:S(2)}) %copy-start) | copy-done | bytes 393240
  1.6 0.0 copy-start.1
  1.6 0.9 %copy-done.1 = s32[16,8,256]{2,1,0:T(8,128)S(1)} copy-done((s32[16,8,256]{2,1,0:T(8,128)S(1)}, s32[16,8,256]{2,1,0:T(8,128)}, u32[]{:S(2)}) %copy-start.1) | copy-done | bytes 131096
  2.5 58.2 %cg.1 = (f32[3,16,8,256]{3,2,1,0:T(8,128)S(1)}, f32[3,16,8,256]{3,2,1,0:T(8,128)S(1)}) custom-call(f32[3,16,8,256]{3,2,1,0:T(8,128)S(1)} %copy-done, s32[16,8,256]{2,1,0:T(8,128)S(1)} %copy-done.1), custom_call_target="tpu_custom_call" | custom-call | tf_op jit(solution)/shard_map/cg/pallas_call | solution.py:419
  60.7 0.7 %copy.6 = f32[3,16,8,256]{3,2,1,0:T(8,128)} copy(f32[3,16,8,256]{3,2,1,0:T(8,128)S(1)} %get-tuple-element.4) | data formatting | bytes 786432
  61.5 0.7 %copy.7 = f32[3,16,8,256]{3,2,1,0:T(8,128)} copy(f32[3,16,8,256]{3,2,1,0:T(8,128)S(1)} %get-tuple-element.5) | data formatting | bytes 786432
Async XLA Ops:
  0.6 1.0 %copy-start = (f32[3,16,8,256]{3,2,1,0:T(8,128)S(1)}, f32[3,16,8,256]{3,2,1,0:T(8,128)}, u32[]{:S(2)}) copy-start(f32[3,16,8,256]{3,2,1,0:T(8,128)} %rhs_hbm.1) | copy-start | bytes 1179652
  1.6 0.9 %copy-start.1 = (s32[16,8,256]{2,1,0:T(8,128)S(1)}, s32[16,8,256]{2,1,0:T(8,128)}, u32[]{:S(2)}) copy-start(s32[16,8,256]{2,1,0:T(8,128)} %lab_hbm.1) | copy-start | bytes 393220

commit v2 on v1

--- a/solution.py
+++ b/solution.py
@@ -115,6 +115,17 @@
     return low, high
 
 
+def loop(first, last, body, init, by):
+    by = math.gcd(last - first, by)
+
+    def trip(k, carry):
+        for step in range(by):
+            carry = body(first + k * by + step, carry)
+        return carry
+
+    return lax.fori_loop(0, (last - first) // by, trip, init)
+
+
 def cg_kernel(nx, ny, cx, cy, nz, rhs_hbm, lab_hbm, sol_ref, res_ref,
               bvec, zvec, vvec, lab, stiff, rinv, comb, forc, ysend, yrecv, csend, crecv,
               psend, precv, in_sem, send_sem, recv_sem, lsend_sem, lrecv_sem,
@@ -184,7 +195,7 @@
                     vec[c, i + 1, pl.ds(row_of[side], 1), :] = yrecv[turn, k, c, pl.ds(i, 1), :]
             return 0
 
-        lax.fori_loop(0, cx, body, 0)
+        loop(0, cx, body, 0, 8)
         for k, (dx, dy) in enumerate(corners):
             for c in range(3):
                 vec[c, plane_of[dx], pl.ds(row_of[dy], 1), :] = crecv[turn, k, pl.ds(c, 1), :]
@@ -199,7 +210,7 @@
         stiff[i + 2, pl.ds(0, cy), :] = lab[i + 2, pl.ds(0, cy), :].astype(F32)
         return 0
 
-    lax.fori_loop(0, cx, pack_first, 0)
+    loop(0, cx, pack_first, 0, 4)
 
     def label_spots(dx, dy):
         planes = ((cx, 0), (cx + 1, 1)) if dx == 1 else ((2, cx + 2),)
@@ -231,7 +242,7 @@
         stiff[i + 2, pl.ds(cy, 1), :] = yrecv[0, 1, 3, pl.ds(i, 1), :]
         return 0
 
-    lax.fori_loop(0, cx, unpack_labels, 0)
+    loop(0, cx, unpack_labels, 0, 8)
     for k, (dx, dy) in enumerate(corners):
         for e, (p, q) in enumerate(label_spots(dx, dy)):
             stiff[p[1], pl.ds(q[1], 1), :] = crecv[0, k, pl.ds(3 + e, 1), :]
@@ -248,7 +259,29 @@
             zvec[0, c, i] = bvec[c, i] * inverse
         return 0
 
-    lax.fori_loop(0, cx + 2, prepare, 0)
+    loop(0, cx + 2, prepare, 0, 3)
+
+    pairs, sums = [], []
+
+    def add_products(turn):
+        def products(i, carry):
+            carry = list(carry)
+            for c in range(3):
+                right = bvec[c, i + 1, pl.ds(0, cy), :]
+                image = vvec[turn, c, i]
+                for k in range(turn + 2):
+                    if k <= turn:
+                        term = zvec[k, c, i + 1, pl.ds(0, cy), :] * image
+                    else:
+                        term = zvec[turn, c, i + 1, pl.ds(0, cy), :] * right
+                    for ty in range(cy // 8):
+                        for tz in range(nz // 128):
+                            carry[k] += term[8 * ty : 8 * ty + 8, 128 * tz : 128 * tz + 128]
+            return tuple(carry)
+
+        zero = jnp.zeros((8, 128), F32)
+        sums.extend(loop(0, cx, products, (zero,) * (turn + 2), 2))
+        pairs.extend([(k, turn) for k in range(turn + 1)] + [(turn, None)])
 
     for turn in range(ITERS):
         def combine(i, _):
@@ -263,7 +296,7 @@
                 comb[i, 4 * c + 3] = d_up - d
             return 0
 
-        lax.fori_loop(0, cx + 2, combine, 0)
+        loop(0, cx + 2, combine, 0, 3)
 
         for ty in range(rows // 8):
             for tz in range(nz // 128):
@@ -284,7 +317,7 @@
                         forc[(p - 1, m) + tile] = before[m] + low[m]
                     return tuple(upper) + tuple(high)
 
-                lax.fori_loop(1, cx + 1, sweep, tuple(second) + tuple(high))
+                loop(1, cx + 1, sweep, tuple(second) + tuple(high), 4)
 
         def finish(i, _):
             for c in range(3):
@@ -304,7 +337,7 @@
                     ysend[turn + 1, 1, c, pl.ds(i, 1), :] = new[:1]
             return 0
 
-        lax.fori_loop(0, cx, finish, 0)
+        loop(0, cx, finish, 0, 4)
         if turn + 1 < ITERS:
             vec = zvec.at[turn + 1]
             for k, (dx, dy) in enumerate(corners):
@@ -312,31 +345,12 @@
                 for c in range(3):
                     csend[turn + 1, k, pl.ds(c, 1), :] = vec[c, plane, pl.ds(line, 1), :]
             arriving = exchange(turn + 1, vec, (3, 3))
+            add_products(turn)
             for copy in arriving:
                 copy.wait_recv()
             unpack(turn + 1, vec)
 
-    pairs = [(i, None) for i in range(ITERS)]
-    pairs += [(i, j) for j in range(ITERS) for i in range(j + 1)]
-
-    def products(i, carry):
-        carry = list(carry)
-        for c in range(3):
-            zs = [zvec[j, c, i + 1, pl.ds(0, cy), :] for j in range(ITERS)]
-            vs = [vvec[j, c, i] for j in range(ITERS)]
-            right = bvec[c, i + 1, pl.ds(0, cy), :]
-            for k, (a, b) in enumerate(pairs):
-                term = zs[a] * (right if b is None else vs[b])
-                part = term[:8, :128]
-                for ty in range(cy // 8):
-                    for tz in range(nz // 128):
-                        if ty or tz:
-                            part = part + term[8 * ty : 8 * ty + 8, 128 * tz : 128 * tz + 128]
-                carry[k] = carry[k] + part
-        return tuple(carry)
-
-    sums = lax.fori_loop(0, cx, products,
-                         tuple(jnp.zeros((8, 128), F32) for _ in pairs))
+    add_products(ITERS - 1)
     lane = lax.broadcasted_iota(jnp.int32, (1, 128), 1)
     row = jnp.zeros((1, 128), F32)
     for k, part in enumerate(sums):
@@ -405,7 +419,7 @@
             res_ref[c, i] = r
         return 0
 
-    lax.fori_loop(0, cx, write, 0)
+    loop(0, cx, write, 0, 4)
 
 
 def solution(mesh):

time: 62.4 us -> 52 us (0.83)
  Pallas kernels: 58.2 us -> 47.8 us
    pallas_call x1, Pallas kernels: 58.2 us -> 47.8 us  [local(): pl.pallas_call(functools.partial(cg_kernel, nx, ny, cx, cy, nz), out_shap...]
where the time goes in v2:
time: 52 us; the launch traced here: 51.8 us
  Pallas kernels  47.8 us (92%)
  local copies, waits for them, and re-layouts  3.39 us (7%)
  between operations  0.65 us (1%)
    pallas_call x1, Pallas kernels, local(): pl.pallas_call(functools.partial(cg_kernel, nx, ny, cx, cy, nz), out_shap...  47.8 us
    unnamed x6, local copies, waits for them, and re-layouts  3.39 us

profile of v2, /device:TPU:0, one launch (start us, length us, event | category | flops | bytes accessed | tf_op | source)
XLA Modules:
  0.0 51.8 jit_solution(12310473486325113669)
XLA Ops:
  0.6 0.0 copy-start
  0.6 1.0 %copy-done = f32[3,16,8,256]{3,2,1,0:T(8,128)S(1)} copy-done((f32[3,16,8,256]{3,2,1,0:T(8,128)S(1)}, f32[3,16,8,256]{3,2,1,0:T(8,128)}, u32[]{:S(2)}) %copy-start) | copy-done | bytes 393240
  1.6 0.0 copy-start.1
  1.6 0.9 %copy-done.1 = s32[16,8,256]{2,1,0:T(8,128)S(1)} copy-done((s32[16,8,256]{2,1,0:T(8,128)S(1)}, s32[16,8,256]{2,1,0:T(8,128)}, u32[]{:S(2)}) %copy-start.1) | copy-done | bytes 131096
  2.5 47.8 %cg.1 = (f32[3,16,8,256]{3,2,1,0:T(8,128)S(1)}, f32[3,16,8,256]{3,2,1,0:T(8,128)S(1)}) custom-call(f32[3,16,8,256]{3,2,1,0:T(8,128)S(1)} %copy-done, s32[16,8,256]{2,1,0:T(8,128)S(1)} %copy-done.1), custom_call_target="tpu_custom_call" | custom-call | tf_op jit(solution)/shard_map/cg/pallas_call | solution.py:433
  50.3 0.7 %copy.6 = f32[3,16,8,256]{3,2,1,0:T(8,128)} copy(f32[3,16,8,256]{3,2,1,0:T(8,128)S(1)} %get-tuple-element.4) | data formatting | bytes 786432
  51.1 0.7 %copy.7 = f32[3,16,8,256]{3,2,1,0:T(8,128)} copy(f32[3,16,8,256]{3,2,1,0:T(8,128)S(1)} %get-tuple-element.5) | data formatting | bytes 786432
Async XLA Ops:
  0.6 1.0 %copy-start = (f32[3,16,8,256]{3,2,1,0:T(8,128)S(1)}, f32[3,16,8,256]{3,2,1,0:T(8,128)}, u32[]{:S(2)}) copy-start(f32[3,16,8,256]{3,2,1,0:T(8,128)} %rhs_hbm.1) | copy-start | bytes 1179652
  1.6 0.9 %copy-start.1 = (s32[16,8,256]{2,1,0:T(8,128)S(1)}, s32[16,8,256]{2,1,0:T(8,128)}, u32[]{:S(2)}) copy-start(s32[16,8,256]{2,1,0:T(8,128)} %lab_hbm.1) | copy-start | bytes 393220
